TPU v7x, 128 devices: a whole 4x4x4 slice. The times are simulated.
128 devices in a mesh: grp: 2 (over core), dev: 64 (over x, y, z).
Axes of the slice: x: 4, y: 4, z: 4, core: 2. Of those that a mesh axis runs over, the one named last changes fastest.
Arguments:
- residual_in: bfloat16 [2048, 2048], P(('grp', 'dev')), may hold values from -1.5 to 1.5
- queries: bfloat16 [2, 1024, 4096], P(None, 'dev', 'grp'), may hold values from -2.5 to 2.5
- latest_key_value: bfloat16 [2, 1024, 4, 256], P(None, 'dev', 'grp'), may hold values from -2.5 to 2.5
- key_value_cache: bfloat16 [2, 1024, 4, 256, 256], P(None, 'dev', 'grp'), may hold values from -2.5 to 2.5
- cache_len: int32 [2, 1024], P(None, 'dev'), may hold values from 1 to 256, 131072 in all within a row
- out_weight: bfloat16 [4096, 2048], P('grp'), may hold values from -0.09375 to 0.09375
- norm_gain: bfloat16 [2048], replicated, may hold values from 0.099609375 to 1.8984375
- router_weight: bfloat16 [2048, 128], replicated, may hold values from -0.125 to 0.125
- routes: int32 [2048, 8], P(('grp', 'dev')), may hold values from 0 to 127, all different within a row; in each aligned block of 16 rows (0 to 15, 16 to 31, ...) at most 2 rows name the same one
- expert_gate_up: bfloat16 [128, 2048, 1536], P(('grp', 'dev')), may hold values from -0.125 to 0.125
- expert_down: bfloat16 [128, 768, 2048], P(('grp', 'dev')), may hold values from -0.21875 to 0.21875
Outputs:
- layer_out: bfloat16 [2048, 2048], P(('grp', 'dev'))
Inputs may be any that keep to these rules, and one draw needn't show every extreme that they name: Each row of cache_len of 1024 entries sums to 131072, and its largest entry is exactly 256. `routes`: the 8 experts of a row are distinct; in each aligned block of 16 rows (the rows of one device) no expert is named by more than 2 rows, a bound that some block reaches.
All inputs are finite; a program needn't handle non-finite values. No bound on the sum of `cache_len` on one device may be relied on, other than what follows from the above.
Results may differ from a plain program's by a relative error of at most 0.017.
Values may be sent and summed in bfloat16 or wider, within the bound.
No kernel may reach another device: no remote copies, remote signals or barrier semaphores. Data moves between devices by JAX's collectives and lax.ppermute only.
A program may use at most 128 MiB of HBM per device.

v0:
```python
import math
import jax
import jax.numpy as jnp
from jax import lax
from jax.sharding import PartitionSpec as P

HEAD_SIZE = 128
FF = 768


def per_device(
    residual_in,
    queries,
    latest_key_value,
    key_value_cache,
    cache_len,
    out_weight,
    norm_gain,
    router_weight,
    routes,
    expert_gate_up,
    expert_down,
):
    halves = queries.shape[0]
    tokens = queries.shape[1]
    kv_heads = key_value_cache.shape[2]
    positions = key_value_cache.shape[3]
    q_heads = queries.shape[2] // HEAD_SIZE
    query_group = q_heads // kv_heads
    width = residual_in.shape[1]
    scale = 1.0 / math.sqrt(HEAD_SIZE)
    query_vector = queries.reshape(halves, tokens, kv_heads, query_group, HEAD_SIZE)
    scores = (
        jnp.einsum(
            "hrkgd,hrksd->hrkgs",
            query_vector,
            key_value_cache[..., :HEAD_SIZE],
            preferred_element_type=jnp.float32,
        )
        * scale
    )
    own_score = (
        jnp.einsum(
            "hrkgd,hrkd->hrkg",
            query_vector,
            latest_key_value[..., :HEAD_SIZE],
            preferred_element_type=jnp.float32,
        )
        * scale
    )
    visible = (
        jnp.arange(positions, dtype=jnp.int32)[None, None, None, None, :]
        < cache_len[:, :, None, None, None]
    )
    raised = jnp.where(visible, jnp.exp(scores), 0.0)
    own_raised = jnp.exp(own_score)
    totals = jnp.sum(raised, axis=-1) + own_raised
    weights = (raised / totals[..., None]).astype(jnp.bfloat16)
    own_weight = (own_raised / totals).astype(jnp.bfloat16)
    mixed = jnp.einsum(
        "hrkgs,hrksd->hrkgd",
        weights,
        key_value_cache[..., HEAD_SIZE:],
        preferred_element_type=jnp.float32,
    )
    mixed = (
        mixed
        + own_weight.astype(jnp.float32)[..., None]
        * latest_key_value[..., HEAD_SIZE:].astype(jnp.float32)[:, :, :, None, :]
    )
    attended = mixed.astype(jnp.bfloat16).reshape(halves * tokens, q_heads * HEAD_SIZE)
    partial_value = jnp.dot(attended, out_weight, preferred_element_type=jnp.float32).reshape(
        halves, tokens, width
    )
    summed = lax.psum(partial_value, "grp")
    projected = lax.dynamic_index_in_dim(summed, lax.axis_index("grp"), 0, keepdims=False)
    hidden = residual_in.astype(jnp.float32) + projected
    meansq = jnp.mean(hidden * hidden, axis=-1, keepdims=True)
    normed = (hidden * lax.rsqrt(meansq + 1e-06) * norm_gain.astype(jnp.float32)).astype(
        jnp.bfloat16
    )
    logits = jnp.dot(normed, router_weight, preferred_element_type=jnp.float32)
    picked = jnp.exp(jnp.take_along_axis(logits, routes, axis=1))
    gates = picked / jnp.sum(picked, axis=1, keepdims=True)
    batch_rows = routes.shape[0]
    topk = routes.shape[1]
    experts_all = router_weight.shape[1]
    capacity = max(2, 2 * batch_rows * topk // experts_all)
    flat_routes = routes.reshape(batch_rows * topk)
    onehot = (flat_routes[:, None] == jnp.arange(experts_all, dtype=jnp.int32)[None, :]).astype(
        jnp.int32
    )
    ranks = jnp.sum(onehot * (jnp.cumsum(onehot, axis=0) - 1), axis=1)
    target = flat_routes * capacity + ranks
    selector = (
        target[None, :] == jnp.arange(experts_all * capacity, dtype=jnp.int32)[:, None]
    ).astype(jnp.int32)
    selector = jnp.sum(selector.reshape(experts_all * capacity, batch_rows, topk), axis=2).astype(
        jnp.bfloat16
    )
    outgoing = jnp.dot(selector, normed, preferred_element_type=jnp.float32).astype(jnp.bfloat16)
    outgoing = outgoing.reshape(experts_all, capacity, width)
    received = lax.all_to_all(outgoing, ("grp", "dev"), split_axis=0, concat_axis=0, tiled=True)
    count = received.shape[0] * received.shape[1]
    gate_up = jnp.dot(
        received.reshape(count, width), expert_gate_up[0], preferred_element_type=jnp.float32
    )
    active = (jax.nn.silu(gate_up[:, :FF]) * gate_up[:, FF:]).astype(jnp.bfloat16)
    result = jnp.dot(active, expert_down[0], preferred_element_type=jnp.float32).astype(
        jnp.bfloat16
    )
    returned = lax.all_to_all(
        result.reshape(received.shape), ("grp", "dev"), split_axis=0, concat_axis=0, tiled=True
    )
    table = returned.reshape(experts_all * capacity, width)
    gathered = table[target].reshape(batch_rows, topk, width).astype(jnp.float32)
    combined = jnp.sum(gates[:, :, None] * gathered, axis=1)
    return (hidden + combined).astype(jnp.bfloat16)


def solution(mesh):
    placed = (
        P(("grp", "dev"), None),
        P(None, "dev", "grp"),
        P(None, "dev", "grp", None),
        P(None, "dev", "grp", None, None),
        P(None, "dev"),
        P("grp", None),
        P(),
        P(),
        P(("grp", "dev"), None),
        P(("grp", "dev"), None, None),
        P(("grp", "dev"), None, None),
    )
    return jax.shard_map(
        per_device, mesh=mesh, in_specs=placed, out_specs=P(("grp", "dev"), None), check_vma=False
    )
```

profile of v0, /device:TPU:0, one launch (start us, length us, event | category | flops | bytes accessed | tf_op | source)
XLA Modules:
  0.0 132.5 jit_solution(18427662515495649888)
XLA Ops:
  6.5 0.0 copy-start
  6.5 0.0 all-reduce.2.cloned.1.call-start
  6.5 0.9 iota_compare_fusion.2
  7.4 0.8 slice_convert_fusion
  8.3 0.9 copy.29
  9.2 0.2 fusion.34
  9.4 3.5 %fusion.43 = (f32[2,16,2,8]{3,2,1,0:T(2,128)S(1)}, f32[2,16,2,8,256]{4,3,2,1,0:T(8,128)S(1)}) fusion(bf16[2,16,2,8,128]{4,3,2,1,0:T(8,128)(2,1)S(1)} %bitcast.50, bf16[2,16,2,256,256]{4,3,2,1,0:T(8,128)(2,1)} %param.14, pred[2,16,256]{2,1,0:T(8,128)(4,1)S(1)} %iota_compare_fusion.2), kind=kOutput, calls=%fused_computation.58 | convolution fusion | flops 33947136 | bytes 4859904 | tf_op jit(solution)/shard_map/hrkgd,hrksd->hrkgs/dot_general | solution.py:34
  12.9 2.9 %fusion.25 = bf16[2,16,2,8,128]{4,3,2,1,0:T(8,128)(2,1)S(1)} fusion(bf16[2,16,2,256,256]{4,3,2,1,0:T(8,128)(2,1)} %param.14, f32[2,16,2,8,256]{4,3,2,1,0:T(8,128)S(1)} %get-tuple-element.12, f32[2,16,2,8]{3,2,1,0:T(2,128)S(1)} %get-tuple-element.6, f32[2,16,2,128]{3,2,1,0:T(2,128)S(1)} %get-tuple-element.7, f32[2,16,2,8]{3,2,1,0:T(2,128)S(1)} %get-tuple-element.5), kind=kOutput, calls=%fused_computation.18 | convolution fusion | flops 34013184 | bytes 4886528 | tf_op jit(solution)/shard_map/hrkgs,hrksd->hrkgd/dot_general | solution.py:60
  15.9 0.1 dot_general.29
  15.9 0.0 copy-start.3
  16.0 0.0 copy-start.4
  16.0 0.0 copy-start.2
  16.0 5.7 %fusion = f32[2,16,2048]{2,1,0:T(8,128)} fusion(bf16[2,16,2048]{2,1,0:T(8,128)(2,1)S(1)} %dot_general.29, bf16[2048,2048]{1,0:T(8,128)(2,1)} %param.16), kind=kOutput, calls=%fused_computation.2 | convolution fusion | flops 268435456 | bytes 8781824 | tf_op jit(solution)/shard_map/dot_general | solution.py:72
  21.6 0.0 all-reduce.2.cloned.1.call-update
  21.7 0.1 copy.25
  21.7 0.1 eq.29
  21.8 0.0 copy-done.4
  21.9 0.1 fusion.33
  21.9 0.2 reduce_window_sum.11
  22.1 0.2 select_reduce_fusion
  22.3 0.1 reduce_sum.62
  22.4 0.1 convert_reduce_fusion
  22.5 25.6 %all-reduce.2.cloned.1.call-done = f32[2,16,2048]{2,1,0:T(8,128)} async-done(((f32[2,16,2048]{2,1,0:T(8,128)}), f32[2,16,2048]{2,1,0:T(8,128)}) %all-reduce.2.cloned.1.call-update) | async-done | bytes 262160 | tf_op jit(solution)/shard_map/psum | solution.py:75
  48.1 1.0 multiply_reduce_fusion
  49.1 1.0 multiply_convert_fusion
  50.1 1.5 %convolution_convert_fusion = bf16[256,2048]{1,0:T(8,128)(2,1)} fusion(bf16[16,2048]{1,0:T(8,128)(2,1)S(1)} %multiply_convert_fusion, s32[256,16]{0,1:T(8,128)S(1)} %convert_reduce_fusion), kind=kOutput, calls=%fused_computation.13 | convolution fusion | flops 17305600 | bytes 1130496 | tf_op jit(solution)/shard_map/dot_general | solution.py:101
  51.6 2.5 %reshape.112 = bf16[128,2,2048]{2,1,0:T(2,128)(2,1)} reshape(bf16[256,2048]{1,0:T(8,128)(2,1)} %convolution_convert_fusion) | data formatting | bytes 2097152 | tf_op jit(solution)/shard_map/reshape | solution.py:102
  54.2 28.3 %all_to_all.10 = bf16[128,2,2048]{2,1,0:T(2,128)(2,1)} all-to-all(bf16[128,2,2048]{2,1,0:T(2,128)(2,1)} %reshape.112), channel_id=1, replica_groups=mesh['grp'=2,'dev'=64] {'grp','dev'}, dimensions={0} | all-to-all | bytes 2097152 | tf_op jit(solution)/shard_map/all_to_all | solution.py:103
  82.4 2.3 %reshape.113 = bf16[256,2048]{1,0:T(8,128)(2,1)} reshape(bf16[128,2,2048]{2,1,0:T(2,128)(2,1)} %all_to_all.10) | data formatting | bytes 2097152 | tf_op jit(solution)/shard_map/reshape | solution.py:106
  84.7 4.9 %fusion.2 = f32[256,1536]{1,0:T(8,128)S(1)} fusion(bf16[256,2048]{1,0:T(8,128)(2,1)} %reshape.113, bf16[1,2048,1536]{2,1,0:T(8,128)(2,1)} %param.20), kind=kOutput, calls=%fused_computation.4 | convolution fusion | flops 1610612736 | bytes 8912896 | tf_op jit(solution)/shard_map/dot_general | solution.py:105
  89.6 2.0 %fusion.10 = bf16[256,2048]{1,0:T(8,128)(2,1)} fusion(bf16[1,768,2048]{2,1,0:T(8,128)(2,1)S(1)} %copy-done, f32[256,1536]{1,0:T(8,128)S(1)} %fusion.2), kind=kOutput, calls=%fused_computation.12 | convolution fusion | flops 807010304 | bytes 5767168 | tf_op jit(solution)/shard_map/dot_general | solution.py:109
  91.7 2.5 %reshape.114 = bf16[128,2,2048]{2,1,0:T(2,128)(2,1)} reshape(bf16[256,2048]{1,0:T(8,128)(2,1)} %fusion.10) | data formatting | bytes 2097152 | tf_op jit(solution)/shard_map/reshape | solution.py:113
  94.2 5.8 %all-to-all-start.1 = ((bf16[128,2,2048]{2,1,0:T(2,128)(2,1)}), bf16[128,2,2048]{2,1,0:T(2,128)(2,1)}, u32[]{:S(2)}, u32[]{:S(2)}) async-start(bf16[128,2,2048]{2,1,0:T(2,128)(2,1)} %reshape.114), calls=%async_computation.1 | async-start | bytes 2097152 | tf_op jit(solution)/shard_map/all_to_all | solution.py:112
  100.0 0.1 copy.22
  100.1 0.1 reshape.125
  100.2 0.1 mul.100
  100.3 1.2 fusion.44
  101.5 1.3 gather_fusion.1
  102.8 0.0 copy-start.1
  102.8 0.1 reshape.128
  102.9 0.1 copy.23
  103.0 0.1 copy.24
  103.0 14.6 %all-to-all-done.1 = bf16[128,2,2048]{2,1,0:T(2,128)(2,1)} async-done(((bf16[128,2,2048]{2,1,0:T(2,128)(2,1)}), bf16[128,2,2048]{2,1,0:T(2,128)(2,1)}, u32[]{:S(2)}, u32[]{:S(2)}) %all-to-all-start.1) | async-done | bytes 1048608 | tf_op jit(solution)/shard_map/all_to_all | solution.py:112
  117.7 2.3 %reshape.115 = bf16[256,2048]{1,0:T(8,128)(2,1)} reshape(bf16[128,2,2048]{2,1,0:T(2,128)(2,1)} %all-to-all-done.1) | data formatting | bytes 2097152 | tf_op jit(solution)/shard_map/reshape | solution.py:115
  119.9 3.6 %gather_fusion = bf16[128,2048]{1,0:T(8,128)(2,1)} fusion(bf16[256,2048]{1,0:T(8,128)(2,1)} %reshape.115, s32[1024]{0:T(1024)S(1)} %pad_clamp_fusion), kind=kCustom, calls=%fused_computation | custom fusion | bytes 1049088 | tf_op jit(solution)/shard_map/gather | solution.py:116
  123.5 1.5 %fusion.28 = f32[16,2048]{1,0:T(8,128)S(1)} fusion(bf16[128,2048]{1,0:T(8,128)(2,1)} %gather_fusion, f32[16,8]{1,0:T(8,128)S(1)} %copy.24), kind=kLoop, calls=%fused_computation.20 | loop fusion | flops 753664 | bytes 655872 | tf_op jit(solution)/shard_map/reduce_sum | solution.py:117
  125.0 0.0 copy-done.1
  125.0 0.7 add_convert_fusion
  (12 shorter events, 0.1 us)
Async XLA Ops:
  6.5 83.1 %copy-start = (bf16[1,768,2048]{2,1,0:T(8,128)(2,1)S(1)}, bf16[1,768,2048]{2,1,0:T(8,128)(2,1)}, u32[]{:S(2)}) copy-start(bf16[1,768,2048]{2,1,0:T(8,128)(2,1)} %param.21) | copy-start | bytes 9437188
  6.5 41.5 %all-reduce.2.cloned.1.call-start = ((), (), s32[]{:S(2)}) async-start(), calls=%async_computation.2 | async-start | bytes 524288 | tf_op jit(solution)/shard_map/psum | solution.py:75
  15.9 5.7 %copy-start.3 = (s32[16,8]{0,1:T(8,128)S(1)}, s32[16,8]{0,1:T(8,128)}, u32[]{:S(2)}) copy-start(s32[16,8]{0,1:T(8,128)} %param.19) | copy-start | bytes 1540
  16.0 5.9 %copy-start.4 = (bf16[2048]{0:T(1024)(128)(2,1)S(1)}, bf16[2048]{0:T(1024)(128)(2,1)}, u32[]{:S(2)}) copy-start(bf16[2048]{0:T(1024)(128)(2,1)} %param.17) | copy-start | bytes 12292
  16.0 32.1 %copy-start.2 = (bf16[16,2048]{1,0:T(8,128)(2,1)S(1)}, bf16[16,2048]{1,0:T(8,128)(2,1)}, u32[]{:S(2)}) copy-start(bf16[16,2048]{1,0:T(8,128)(2,1)} %param.11) | copy-start | bytes 196612
  94.2 23.5 %all-to-all-start.1 = ((bf16[128,2,2048]{2,1,0:T(2,128)(2,1)}), bf16[128,2,2048]{2,1,0:T(2,128)(2,1)}, u32[]{:S(2)}, u32[]{:S(2)}) async-start(bf16[128,2,2048]{2,1,0:T(2,128)(2,1)} %reshape.114), calls=%async_computation.1 | async-start | bytes 2097152 | tf_op jit(solution)/shard_map/all_to_all | solution.py:112
  102.8 22.3 %copy-start.1 = (f32[2,16,2048]{2,1,0:T(8,128)S(1)}, f32[2,16,2048]{2,1,0:T(8,128)}, u32[]{:S(2)}) copy-start(f32[2,16,2048]{2,1,0:T(8,128)} %all-reduce.2.cloned.1.call-done) | copy-start | bytes 786436
Sparse Core Ops, SparseCore 0:
  21.8 26.2 all-reduce.1
where the time goes:
time: 133 us
  waiting for transfers between devices  40.2 us (30%)
  blocking collectives  28.3 us (21%)
  matrix products  21.9 us (16%)
  local copies, waits for them, and re-layouts  16.2 us (12%)
  between operations  13.6 us (10%)
  other arithmetic  6.56 us (5%)
  starting transfers between devices  5.78 us (4%)
    all_to_all x1, blocking collectives, per_device(): lax.all_to_all(outgoing, ('grp', 'dev'), split_axis=0, concat_axis=0, til...  28.3 us
    psum x1, waiting for transfers between devices, per_device(): summed = lax.psum(partial_value, 'grp')  25.6 us
    all_to_all x1, waiting for transfers between devices, per_device(): lax.all_to_all(result.reshape(received.shape), ('grp', 'dev'), split_axis...  14.6 us
    all_to_all x1, starting transfers between devices, per_device(): lax.all_to_all(result.reshape(received.shape), ('grp', 'dev'), split_axis...  5.78 us
    dot_general x1, matrix products, per_device(): jnp.dot(attended, out_weight, preferred_element_type=jnp.float32)  5.65 us
    dot_general x1, matrix products, per_device(): jnp.dot(received.reshape(count, width), expert_gate_up[0], preferred_elem...  4.9 us
    gather x1, local copies, waits for them, and re-layouts, per_device(): table[target].reshape(batch_rows, topk, width).astype(jnp.float32)  3.59 us
    dot_general x1, matrix products, per_device(): jnp.einsum('hrkgd,hrksd->hrkgs', query_vector, key_value_cache[..., :HEAD...  3.5 us
  transfers between devices with their start and end apart: 2, of which 2 were waited for; matrix products, arithmetic and copies ran while one was open for 3% of the time, Pallas kernels for 0%

commit v1 on v0

--- a/solution.py
+++ b/solution.py
@@ -72,7 +72,7 @@
     partial_value = jnp.dot(attended, out_weight, preferred_element_type=jnp.float32).reshape(
         halves, tokens, width
     )
-    summed = lax.psum(partial_value, "grp")
+    summed = jnp.sum(lax.all_gather(partial_value, "grp"), axis=0)
     projected = lax.dynamic_index_in_dim(summed, lax.axis_index("grp"), 0, keepdims=False)
     hidden = residual_in.astype(jnp.float32) + projected
     meansq = jnp.mean(hidden * hidden, axis=-1, keepdims=True)

time: 133 us -> 101 us (0.76)
  waiting for transfers between devices: 40.2 us -> 13.4 us
  between operations: 13.6 us -> 0.19 us
  blocking collectives: 28.3 us -> 31.7 us
  local copies, waits for them, and re-layouts: 16.2 us -> 18.8 us
  other arithmetic: 6.56 us -> 8.85 us
    psum x1 -> x0, waiting for transfers between devices: 25.6 us -> none  [per_device(): summed = lax.psum(partial_value, 'grp')]
    all_gather x0 -> x1, blocking collectives: none -> 2.31 us  [per_device(): summed = jnp.sum(lax.all_gather(partial_value, 'grp'), axis=0)]
    unnamed x12 -> x14, local copies, waits for them, and re-layouts: 1.03 us -> 2.4 us
  transfers between devices with their start and end apart: 2 -> 1, of which waited for: 2 -> 1; matrix products, arithmetic and copies ran while one was open for 3% -> 4% of each run, Pallas kernels for 0% -> 0%
where the time goes in v1:
time: 101 us
  blocking collectives  31.7 us (31%)
  matrix products  21.9 us (22%)
  local copies, waits for them, and re-layouts  18.8 us (19%)
  waiting for transfers between devices  13.4 us (13%)
  other arithmetic  8.85 us (9%)
  starting transfers between devices  5.78 us (6%)
    all_to_all x1, blocking collectives, per_device(): lax.all_to_all(outgoing, ('grp', 'dev'), split_axis=0, concat_axis=0, til...  29.4 us
    all_to_all x1, waiting for transfers between devices, per_device(): lax.all_to_all(result.reshape(received.shape), ('grp', 'dev'), split_axis...  13.4 us
    all_to_all x1, starting transfers between devices, per_device(): lax.all_to_all(result.reshape(received.shape), ('grp', 'dev'), split_axis...  5.78 us
    dot_general x1, matrix products, per_device(): jnp.dot(attended, out_weight, preferred_element_type=jnp.float32)  4.95 us
    dot_general x1, matrix products, per_device(): jnp.dot(received.reshape(count, width), expert_gate_up[0], preferred_elem...  4.9 us
    gather x1, local copies, waits for them, and re-layouts, per_device(): table[target].reshape(batch_rows, topk, width).astype(jnp.float32)  3.59 us
    dot_general x1, matrix products, per_device(): jnp.einsum('hrkgd,hrksd->hrkgs', query_vector, key_value_cache[..., :HEAD...  3.5 us
    dot_general x1, matrix products, per_device(): jnp.einsum('hrkgs,hrksd->hrkgd', weights, key_value_cache[..., HEAD_SIZE:...  2.91 us
  transfers between devices with their start and end apart: 1, of which 1 were waited for; matrix products, arithmetic and copies ran while one was open for 4% of the time, Pallas kernels for 0%

profile of v1, /device:TPU:0, one launch (start us, length us, event | category | flops | bytes accessed | tf_op | source)
XLA Modules:
  0.0 100.6 jit_solution(16549710308279374977)
XLA Ops:
  0.0 0.0 copy-start
  0.0 0.9 copy.30
  0.9 0.1 eq.29
  1.0 0.8 iota_compare_fusion.2
  1.8 1.3 %convert_element_type.58 = f32[2048]{0:T(1024)} convert(bf16[2048]{0:T(1024)(128)(2,1)} %param.17) | non-fusion elementwise | flops 2048 | bytes 12288 | tf_op jit(solution)/shard_map/convert_element_type | solution.py:79
  3.0 0.8 slice_convert_fusion
  3.8 0.1 fusion.33
  3.9 0.2 reduce_window_sum.11
  4.1 0.2 select_reduce_fusion
  4.2 0.5 copy-done.3
  4.8 0.1 reduce_sum.72
  4.9 0.6 broadcast_multiply_fusion
  5.5 0.7 convert_reduce_fusion
  6.2 0.9 copy.34
  7.1 0.2 fusion.34
  7.3 3.5 %fusion.43 = (f32[2,16,2,8]{3,2,1,0:T(2,128)S(1)}, f32[2,16,2,8,256]{4,3,2,1,0:T(8,128)S(1)}) fusion(bf16[2,16,2,8,128]{4,3,2,1,0:T(8,128)(2,1)S(1)} %bitcast.52, bf16[2,16,2,256,256]{4,3,2,1,0:T(8,128)(2,1)} %param.14, pred[2,16,256]{2,1,0:T(8,128)(4,1)S(1)} %iota_compare_fusion.2), kind=kOutput, calls=%fused_computation.58 | convolution fusion | flops 33947136 | bytes 4859904 | tf_op jit(solution)/shard_map/hrkgd,hrksd->hrkgs/dot_general | solution.py:34
  10.8 0.1 fusion.37
  10.9 2.9 %fusion.25 = bf16[2,16,2,8,128]{4,3,2,1,0:T(8,128)(2,1)S(1)} fusion(bf16[2,16,2,256,256]{4,3,2,1,0:T(8,128)(2,1)} %param.14, f32[2,16,2,8,256]{4,3,2,1,0:T(8,128)S(1)} %get-tuple-element.12, f32[2,16,2,8]{3,2,1,0:T(2,128)S(1)} %get-tuple-element.6, f32[2,16,2,128]{3,2,1,0:T(2,128)S(1)} %get-tuple-element.7, f32[2,16,2,8]{3,2,1,0:T(2,128)S(1)} %get-tuple-element.5), kind=kOutput, calls=%fused_computation.18 | convolution fusion | flops 34013184 | bytes 4886528 | tf_op jit(solution)/shard_map/hrkgs,hrksd->hrkgd/dot_general | solution.py:60
  13.8 0.1 reshape.115
  13.9 0.0 copy-start.1
  13.9 5.0 %fusion = f32[2,16,2048]{2,1,0:T(8,128)S(1)} fusion(bf16[2,16,2048]{2,1,0:T(8,128)(2,1)S(1)} %reshape.115, bf16[2048,2048]{1,0:T(8,128)(2,1)} %param.16), kind=kOutput, calls=%fused_computation.2 | convolution fusion | flops 268435456 | bytes 8781824 | tf_op jit(solution)/shard_map/dot_general | solution.py:72
  18.8 2.3 %all-gather = f32[4,16,2048]{2,1,0:T(8,128)} all-gather(f32[2,16,2048]{2,1,0:T(8,128)S(1)} %fusion), channel_id=2, replica_groups=mesh['grp'=2,'dev'=64] {'grp'}, dimensions={0}, use_global_device_ids=true | all-gather | bytes 786432 | tf_op jit(solution)/shard_map/all_gather | solution.py:75
  21.1 1.1 %reduce_sum.68 = f32[2,16,2048]{2,1,0:T(8,128)S(1)} reduce(f32[2,2,16,2048]{3,2,1,0:T(8,128)} %bitcast.50, f32[]{:T(128)} %constant.19.clone.1), dimensions={0}, to_apply=%region_1.2 | reduce | flops 65536 | bytes 786436 | tf_op jit(solution)/shard_map/reduce_sum | solution.py:75
  22.3 0.1 multiply_reduce_fusion
  22.4 0.8 multiply_convert_fusion
  23.2 2.2 %convolution_convert_fusion = bf16[256,2048]{1,0:T(8,128)(2,1)} fusion(bf16[16,2048]{1,0:T(8,128)(2,1)S(1)} %multiply_convert_fusion, s32[256,16]{0,1:T(8,128)} %convert_reduce_fusion), kind=kOutput, calls=%fused_computation.13 | convolution fusion | flops 17305600 | bytes 1130496 | tf_op jit(solution)/shard_map/dot_general | solution.py:101
  25.4 2.5 %reshape.117 = bf16[128,2,2048]{2,1,0:T(2,128)(2,1)} reshape(bf16[256,2048]{1,0:T(8,128)(2,1)} %convolution_convert_fusion) | data formatting | bytes 2097152 | tf_op jit(solution)/shard_map/reshape | solution.py:102
  28.0 29.4 %all_to_all.10 = bf16[128,2,2048]{2,1,0:T(2,128)(2,1)} all-to-all(bf16[128,2,2048]{2,1,0:T(2,128)(2,1)} %reshape.117), channel_id=1, replica_groups=mesh['grp'=2,'dev'=64] {'grp','dev'}, dimensions={0} | all-to-all | bytes 2097152 | tf_op jit(solution)/shard_map/all_to_all | solution.py:103
  57.3 2.3 %reshape.118 = bf16[256,2048]{1,0:T(8,128)(2,1)} reshape(bf16[128,2,2048]{2,1,0:T(2,128)(2,1)} %all_to_all.10) | data formatting | bytes 2097152 | tf_op jit(solution)/shard_map/reshape | solution.py:106
  59.6 4.9 %fusion.2 = f32[256,1536]{1,0:T(8,128)S(1)} fusion(bf16[256,2048]{1,0:T(8,128)(2,1)} %reshape.118, bf16[1,2048,1536]{2,1,0:T(8,128)(2,1)} %param.20), kind=kOutput, calls=%fused_computation.4 | convolution fusion | flops 1610612736 | bytes 8912896 | tf_op jit(solution)/shard_map/dot_general | solution.py:105
  64.5 0.0 copy-done
  64.5 0.0 copy-start.2
  64.5 2.0 %fusion.10 = bf16[256,2048]{1,0:T(8,128)(2,1)} fusion(bf16[1,768,2048]{2,1,0:T(8,128)(2,1)S(1)} %copy-done, f32[256,1536]{1,0:T(8,128)S(1)} %fusion.2), kind=kOutput, calls=%fused_computation.12 | convolution fusion | flops 807010304 | bytes 5767168 | tf_op jit(solution)/shard_map/dot_general | solution.py:109
  66.6 2.5 %reshape.119 = bf16[128,2,2048]{2,1,0:T(2,128)(2,1)} reshape(bf16[256,2048]{1,0:T(8,128)(2,1)} %fusion.10) | data formatting | bytes 2097152 | tf_op jit(solution)/shard_map/reshape | solution.py:113
  69.1 5.8 %all-to-all-start.1 = ((bf16[128,2,2048]{2,1,0:T(2,128)(2,1)}), bf16[128,2,2048]{2,1,0:T(2,128)(2,1)}, u32[]{:S(2)}, u32[]{:S(2)}) async-start(bf16[128,2,2048]{2,1,0:T(2,128)(2,1)} %reshape.119), calls=%async_computation.1 | async-start | bytes 2097152 | tf_op jit(solution)/shard_map/all_to_all | solution.py:112
  74.9 0.1 copy.27
  75.0 0.1 reshape.130
  75.1 1.3 %mul.100 = s32[128,1]{0,1:T(1,128)} reshape(s32[16,8]{1,0:T(8,128)} %get-tuple-element.9) | data formatting | bytes 1024 | tf_op jit(solution)/shard_map/mul | solution.py:94
  76.4 1.2 %fusion.44 = f32[16,128]{1,0:T(8,128)S(1)} fusion(bf16[16,2048]{1,0:T(8,128)(2,1)S(1)} %multiply_convert_fusion, bf16[2048,128]{1,0:T(8,128)(2,1)} %param.18), kind=kOutput, calls=%fused_computation.59 | convolution fusion | flops 8388608 | bytes 598016 | tf_op jit(solution)/shard_map/dot_general | solution.py:82
  77.6 1.2 %gather_fusion.1 = f32[128]{0:T(128)S(1)} fusion(f32[16,128]{1,0:T(8,128)S(1)} %fusion.44, s32[128]{0:T(128)S(1)} %reshape.130), kind=kCustom, calls=%fused_computation.1 | custom fusion | bytes 2048 | tf_op jit(solution)/shard_map/jit(take_along_axis)/gather | solution.py:83
  78.9 0.1 reshape.133
  78.9 0.1 copy.28
  79.1 0.1 copy.29
  79.2 13.4 %all-to-all-done.1 = bf16[128,2,2048]{2,1,0:T(2,128)(2,1)} async-done(((bf16[128,2,2048]{2,1,0:T(2,128)(2,1)}), bf16[128,2,2048]{2,1,0:T(2,128)(2,1)}, u32[]{:S(2)}, u32[]{:S(2)}) %all-to-all-start.1) | async-done | bytes 1048608 | tf_op jit(solution)/shard_map/all_to_all | solution.py:112
  92.6 2.3 %reshape.120 = bf16[256,2048]{1,0:T(8,128)(2,1)} reshape(bf16[128,2,2048]{2,1,0:T(2,128)(2,1)} %all-to-all-done.1) | data formatting | bytes 2097152 | tf_op jit(solution)/shard_map/reshape | solution.py:115
  94.8 3.6 %gather_fusion = bf16[128,2048]{1,0:T(8,128)(2,1)} fusion(bf16[256,2048]{1,0:T(8,128)(2,1)} %reshape.120, s32[1024]{0:T(1024)S(1)} %pad_clamp_fusion), kind=kCustom, calls=%fused_computation | custom fusion | bytes 1049088 | tf_op jit(solution)/shard_map/gather | solution.py:116
  98.4 1.5 %fusion.28 = f32[16,2048]{1,0:T(8,128)S(1)} fusion(bf16[128,2048]{1,0:T(8,128)(2,1)} %gather_fusion, f32[16,8]{1,0:T(8,128)S(1)} %copy.29), kind=kLoop, calls=%fused_computation.20 | loop fusion | flops 753664 | bytes 655872 | tf_op jit(solution)/shard_map/reduce_sum | solution.py:117
  99.9 0.7 add_convert_fusion
  (13 shorter events, 0.1 us)
Async XLA Ops:
  0.0 64.5 %copy-start = (bf16[1,768,2048]{2,1,0:T(8,128)(2,1)S(1)}, bf16[1,768,2048]{2,1,0:T(8,128)(2,1)}, u32[]{:S(2)}) copy-start(bf16[1,768,2048]{2,1,0:T(8,128)(2,1)} %param.21) | copy-start | bytes 9437188
  4.2 0.6 copy-start.3
  13.9 8.4 %copy-start.1 = (bf16[16,2048]{1,0:T(8,128)(2,1)S(1)}, bf16[16,2048]{1,0:T(8,128)(2,1)}, u32[]{:S(2)}) copy-start(bf16[16,2048]{1,0:T(8,128)(2,1)} %param.11) | copy-start | bytes 196612
  64.5 10.4 %copy-start.2 = (s32[16,8]{0,1:T(8,128)S(1)}, s32[16,8]{0,1:T(8,128)}, u32[]{:S(2)}) copy-start(s32[16,8]{0,1:T(8,128)} %param.19) | copy-start | bytes 1540
  69.1 23.5 %all-to-all-start.1 = ((bf16[128,2,2048]{2,1,0:T(2,128)(2,1)}), bf16[128,2,2048]{2,1,0:T(2,128)(2,1)}, u32[]{:S(2)}, u32[]{:S(2)}) async-start(bf16[128,2,2048]{2,1,0:T(2,128)(2,1)} %reshape.119), calls=%async_computation.1 | async-start | bytes 2097152 | tf_op jit(solution)/shard_map/all_to_all | solution.py:112
  77.6 1.5 %copy-start.4 = (s32[128]{0:T(128)S(1)}, s32[128]{0:T(128)}, u32[]{:S(2)}) copy-start(s32[128]{0:T(128)} %copy-done.3) | copy-start | bytes 1540
  77.6 1.5 %copy-start.5 = (s32[128,1]{0,1:T(1,128)S(1)}, s32[128,1]{0,1:T(1,128)}, u32[]{:S(2)}) copy-start(s32[128,1]{0,1:T(1,128)} %mul.100) | copy-start | bytes 1540
